TPU v7x, 256 devices: a whole 4x4x8 slice. The times are simulated.
256 devices in a mesh: group: 32 (over x, y, core), tp: 8 (over z).
Axes of the slice: x: 4, y: 4, z: 8, core: 2. Of those that a mesh axis runs over, the one named last changes fastest.
Arguments:
- hidden_in: bfloat16 [64, 3072], P('group'), may hold values from -6 to 6
- w_qkv: bfloat16 [3072, 2048], P(None, 'tp'), may hold values from -0.109375 to 0.109375
- w_out: bfloat16 [1536, 3072], P('tp'), may hold values from -0.15625 to 0.15625
- kv_pool: bfloat16 [2048, 128, 512], P(('group', 'tp'))
- page_table: int32 [64, 32], replicated, may hold values from 0 to 2047, as said below
- lengths: int32 [64], replicated, may hold values from 1 to 4096, as said below
Outputs:
- attn_proj: bfloat16 [64, 3072], P('group', 'tp')
Inputs may be any that keep to these rules, and one draw needn't show every extreme that they name: `page_table`: every pool slot is named by exactly one request page. `lengths`: some request has the full 32 * 128 cached tokens.
All inputs are finite; a program needn't handle non-finite values.
Results may differ from a plain program's by a relative error of at most 0.0085.
The roundings to bfloat16 on the way count: a program that leaves them out, or rounds other values in their place, can miss the bound.
Values may be sent and summed in bfloat16 or wider, within the bound.
A program may use at most 64 MiB of HBM per device.

v0:
```python
import jax
import jax.numpy as jnp
from jax import lax
from jax.sharding import PartitionSpec as P

HEADS = 12
KV_HEADS = 2
HEAD_DIM = 128


def on_device(hidden_in, w_qkv, w_out, kv_pool, page_table, lengths):
    qdim = HEADS * HEAD_DIM
    kdim = KV_HEADS * HEAD_DIM
    per_kv = HEADS // KV_HEADS
    scale = HEAD_DIM ** (-0.5)
    req_grp = hidden_in.shape[0]
    col_count = w_out.shape[0]
    col_start = lax.axis_index("tp") * col_count
    columns = jnp.dot(hidden_in, w_qkv, preferred_element_type=jnp.float32).astype(jnp.bfloat16)
    qkv = lax.all_gather(columns, "tp", axis=1, tiled=True)
    queries = lax.all_gather(qkv[:, :qdim], "group", axis=0, tiled=True)
    requests = queries.shape[0]
    slot_count = kv_pool.shape[0]
    page_len = kv_pool.shape[1]
    max_pages = page_table.shape[1]
    slot_ids = lax.axis_index(("group", "tp")) * slot_count + jnp.arange(
        slot_count, dtype=jnp.int32
    )
    match = page_table[:, :, None] == slot_ids[None, None, :]
    slot_req = jnp.sum(
        jnp.where(match, jnp.arange(requests, dtype=jnp.int32)[:, None, None], 0), axis=(0, 1)
    )
    slot_page = jnp.sum(
        jnp.where(match, jnp.arange(max_pages, dtype=jnp.int32)[None, :, None], 0), axis=(0, 1)
    )
    chosen = queries[slot_req].reshape(slot_count, KV_HEADS, per_kv, HEAD_DIM)
    keys = kv_pool[..., :kdim].reshape(slot_count, page_len, KV_HEADS, HEAD_DIM)
    values = kv_pool[..., kdim:].reshape(slot_count, page_len, KV_HEADS, HEAD_DIM)
    scores = jnp.einsum("pgjd,ptgd->pgjt", chosen, keys, preferred_element_type=jnp.float32) * scale
    position = slot_page[:, None] * page_len + jnp.arange(page_len, dtype=jnp.int32)[None, :]
    live = (position < lengths[slot_req][:, None])[:, None, None, :]
    top = jnp.max(jnp.where(live, scores, -1e30), axis=-1)
    probs = jnp.where(live, jnp.exp(scores - top[..., None]), 0.0).astype(jnp.bfloat16)
    total = jnp.sum(probs.astype(jnp.float32), axis=-1)
    weighted = jnp.einsum("pgjt,ptgd->pgjd", probs, values, preferred_element_type=jnp.float32)
    owner = slot_req[None, :] == jnp.arange(requests, dtype=jnp.int32)[:, None]
    req_top = jnp.max(jnp.where(owner[:, :, None, None], top[None], -1e30), axis=1)
    factor = jnp.exp(top - req_top[slot_req])
    onehot = owner.astype(jnp.float32)
    req_total = jnp.einsum(
        "rp,pgj->rgj", onehot, total * factor, precision=lax.Precision.HIGHEST
    ).reshape(requests, HEADS)
    req_sums = jnp.einsum(
        "rp,pgjd->rgjd", onehot, weighted * factor[..., None], precision=lax.Precision.HIGHEST
    ).reshape(requests, qdim)
    req_top = req_top.reshape(requests, HEADS)
    start = lax.axis_index("group") * req_grp
    peak_all = lax.pmax(req_top, ("group", "tp"))
    rescale = jnp.exp(req_top - peak_all)
    total_all, sums_all = lax.psum(
        (req_total * rescale, req_sums * jnp.repeat(rescale, HEAD_DIM, axis=1)), ("group", "tp")
    )
    peak = lax.dynamic_slice_in_dim(peak_all, start, req_grp, 0)
    whole = lax.dynamic_slice_in_dim(total_all, start, req_grp, 0)
    sums = lax.dynamic_slice_in_dim(sums_all, start, req_grp, 0)
    sums_part = lax.dynamic_slice_in_dim(sums, col_start, col_count, 1)
    own_q = qkv[:, :qdim].reshape(req_grp, KV_HEADS, per_kv, HEAD_DIM)
    own_k = qkv[:, qdim : qdim + kdim].reshape(req_grp, KV_HEADS, HEAD_DIM)
    own_v = qkv[:, qdim + kdim :].reshape(req_grp, KV_HEADS, HEAD_DIM)
    own_score = (
        jnp.einsum("rgjd,rgd->rgj", own_q, own_k, preferred_element_type=jnp.float32) * scale
    ).reshape(req_grp, HEADS)
    own_sums = jnp.broadcast_to(
        own_v.astype(jnp.float32)[:, :, None, :], (req_grp, KV_HEADS, per_kv, HEAD_DIM)
    ).reshape(req_grp, qdim)
    new_peak = jnp.maximum(peak, own_score)
    old_factor = jnp.exp(peak - new_peak)
    own_factor = jnp.exp(own_score - new_peak)
    new_whole = whole * old_factor + own_factor

    def pick(values_full):
        return lax.dynamic_slice_in_dim(values_full, col_start, col_count, 1)

    new_sums = sums_part * pick(jnp.repeat(old_factor, HEAD_DIM, axis=1)) + pick(
        own_sums * jnp.repeat(own_factor, HEAD_DIM, axis=1)
    )
    attn_part = (new_sums / pick(jnp.repeat(new_whole, HEAD_DIM, axis=1))).astype(jnp.bfloat16)
    partial_value = jnp.dot(attn_part, w_out, preferred_element_type=jnp.float32)
    return lax.psum_scatter(partial_value, "tp", scatter_dimension=1, tiled=True).astype(
        jnp.bfloat16
    )


def solution(mesh):
    in_specs = (
        P("group", None),
        P(None, "tp"),
        P("tp", None),
        P(("group", "tp"), None, None),
        P(),
        P(),
    )
    out_specs = P("group", "tp")
    return jax.shard_map(
        on_device, mesh=mesh, in_specs=in_specs, out_specs=out_specs, check_vma=False
    )
```

profile of v0, /device:TPU:2, one launch (start us, length us, event | category | flops | bytes accessed | tf_op | source)
XLA Modules:
  0.0 429.0 jit_solution(9588263399593622062)
XLA Ops:
  6.5 1.1 fusion.1
  7.7 0.2 copy-done
  8.0 1.0 convolution_convert_fusion
  9.0 19.1 %all_gather.6 = bf16[2,2048]{1,0:T(2,128)(2,1)S(1)} all-gather(bf16[2,256]{1,0:T(2,128)(2,1)S(1)} %convolution_convert_fusion), channel_id=1, replica_groups=mesh['group'=32,'tp'=8] {'tp'}, dimensions={1}, use_global_device_ids=true | all-gather | bytes 9216 | tf_op jit(solution)/shard_map/all_gather | solution.py:20
  28.1 24.7 %all-gather = bf16[32,2,1536]{2,1,0:T(2,128)(2,1)S(1)} all-gather(bf16[1,2,1536]{2,1,0:T(2,128)(2,1)S(1)} %get-tuple-element.19), channel_id=1, replica_groups=mesh['group'=32,'tp'=8] {'group'}, dimensions={0}, use_global_device_ids=true | all-gather | bytes 202752 | tf_op jit(solution)/shard_map/all_gather | solution.py:21
  52.9 0.6 gather_fusion
  53.5 0.6 gather_fusion.1
  54.1 1.3 fusion.25
  55.4 0.3 copy.96
  55.8 0.3 select_reduce_fusion
  56.1 0.1 copy.81
  56.2 0.1 select_reduce_fusion.1
  56.3 0.1 copy.82
  56.4 0.3 copy.97
  56.7 0.2 convert_reduce_fusion
  56.9 0.1 copy.86
  57.0 74.0 %pmax.7 = f32[64,12]{1,0:T(8,128)S(1)} all-reduce(f32[64,12]{1,0:T(8,128)S(1)} %copy.86), channel_id=1, replica_groups=mesh['group'=32,'tp'=8] {'group','tp'}, use_global_device_ids=true, to_apply=%region_4.5 | all-reduce | flops 768 | bytes 6144 | tf_op jit(solution)/shard_map/pmax | solution.py:58
  131.0 0.6 gather_fusion.2
  131.6 0.2 fusion.5
  131.8 0.1 copy.88
  131.9 0.4 convolution_multiply_fusion
  132.3 0.4 fusion.2
  132.8 0.2 copy.84
  133.0 0.1 reshape.129
  133.2 0.2 broadcast_in_dim.104
  133.4 0.9 bitcast_multiply_fusion
  134.4 0.1 fusion.27
  134.6 74.9 %psum.15 = f32[64,12]{1,0:T(8,128)S(1)} all-reduce(f32[64,12]{1,0:T(8,128)S(1)} %get-tuple-element.10), channel_id=1, replica_groups=mesh['group'=32,'tp'=8] {'group','tp'}, use_global_device_ids=true, to_apply=%region_7.8 | all-reduce | flops 768 | bytes 6144 | tf_op jit(solution)/shard_map/psum | solution.py:60
  209.7 168.6 %all-reduce.2.cloned.1.call-done = f32[64,1536]{1,0:T(8,128)} async-done(((f32[64,1536]{1,0:T(8,128)}), f32[64,1536]{1,0:T(8,128)}) %all-reduce.2.cloned.1.call-update) | async-done | bytes 393232 | tf_op jit(solution)/shard_map/psum | solution.py:60
  378.3 2.7 convolution_bitcast_fusion
  381.0 39.5 %reduce-scatter.4.cloned.1.call-done = f32[384,2]{1,0:T(8,128)} async-done(((f32[3072,2]{1,0:T(8,128)}), f32[384,2]{1,0:T(8,128)}) %reduce-scatter.4.cloned.1.call-update) | async-done | bytes 3088
  420.5 1.6 copy.95
  (35 shorter events, 0.7 us)
Async XLA Ops:
  6.5 1.4 copy-start
  6.5 46.4 %copy-start.1 = (s32[64]{0:T(128)S(1)}, s32[64]{0:T(128)}, u32[]{:S(2)}) copy-start(s32[64]{0:T(128)} %param.11) | copy-start | bytes 772
  6.5 371.7 %all-reduce.2.cloned.1.call-start = ((), (), s32[]{:S(2)}) async-start(), calls=%async_computation.1 | async-start | bytes 786432 | tf_op jit(solution)/shard_map/psum | solution.py:60
  133.1 245.2 %copy-start.2 = (bf16[192,3072]{1,0:T(8,128)(2,1)S(1)}, bf16[192,3072]{1,0:T(8,128)(2,1)}, u32[]{:S(2)}) copy-start(bf16[192,3072]{1,0:T(8,128)(2,1)} %param.8) | copy-start | bytes 3538948
  134.3 286.2 %reduce-scatter.4.cloned.1.call-start = ((), (), s32[]{:S(2)}) async-start(), calls=%async_computation.2 | async-start | bytes 1769472
Sparse Core Ops, SparseCore 0:
  134.4 243.8 all-reduce.1
  381.1 39.3 reduce-scatter.3
where the time goes:
time: 430 us; the launch traced here: 429 us
  waiting for transfers between devices  208 us (48%)
  blocking collectives  193 us (45%)
  between operations  13.6 us (3%)
  local copies, waits for them, and re-layouts  6.81 us (2%)
  matrix products  5.21 us (1%)
    psum x1, waiting for transfers between devices, on_device(): lax.psum((req_total * rescale, req_sums * jnp.repeat(rescale, HEAD_DIM, a...  169 us
    psum x1, blocking collectives, on_device(): lax.psum((req_total * rescale, req_sums * jnp.repeat(rescale, HEAD_DIM, a...  74.9 us
    pmax x1, blocking collectives, on_device(): peak_all = lax.pmax(req_top, ('group', 'tp'))  74 us
    unnamed x3, waiting for transfers between devices  39.6 us
    all_gather x1, blocking collectives, on_device(): queries = lax.all_gather(qkv[:, :qdim], 'group', axis=0, tiled=True)  24.7 us
    all_gather x1, blocking collectives, on_device(): qkv = lax.all_gather(columns, 'tp', axis=1, tiled=True)  19.1 us
  transfers between devices with their start and end apart: 2, of which 2 were waited for; matrix products, arithmetic and copies ran while one was open for 0% of the time, Pallas kernels for 0%

commit v1 on v0

--- a/solution.py
+++ b/solution.py
@@ -6,6 +6,11 @@
 HEADS = 12
 KV_HEADS = 2
 HEAD_DIM = 128
+
+
+def one_after_other(value, axis_one, axis_two):
+    partial = lax.psum(value, axis_one)
+    return lax.psum(partial, axis_two)
 
 
 def on_device(hidden_in, w_qkv, w_out, kv_pool, page_table, lengths):
@@ -57,8 +62,8 @@
     start = lax.axis_index("group") * req_grp
     peak_all = lax.pmax(req_top, ("group", "tp"))
     rescale = jnp.exp(req_top - peak_all)
-    total_all, sums_all = lax.psum(
-        (req_total * rescale, req_sums * jnp.repeat(rescale, HEAD_DIM, axis=1)), ("group", "tp")
+    total_all, sums_all = one_after_other(
+        (req_total * rescale, req_sums * jnp.repeat(rescale, HEAD_DIM, axis=1)), "tp", "group"
     )
     peak = lax.dynamic_slice_in_dim(peak_all, start, req_grp, 0)
     whole = lax.dynamic_slice_in_dim(total_all, start, req_grp, 0)

time: 430 us -> 445 us (1.035)
  blocking collectives: 193 us -> 253 us
  waiting for transfers between devices: 208 us -> 164 us
    psum x1 -> x2, blocking collectives: 74.9 us -> 135 us  [the longest x1 106 us: one_after_other(): return lax.psum(partial, axis_two)]
    psum x1 -> x2, waiting for transfers between devices: 169 us -> 123 us  [the longest x1 123 us: one_after_other(): return lax.psum(partial, axis_two)]
    unnamed x3 -> x4, waiting for transfers between devices: 39.6 us -> 40.7 us
  transfers between devices with their start and end apart: 2 -> 3, of which waited for: 2 -> 2; matrix products, arithmetic and copies ran while one was open for 0% -> 0% of each run, Pallas kernels for 0% -> 0%
where the time goes in v1:
time: 445 us
  blocking collectives  253 us (57%)
  waiting for transfers between devices  164 us (37%)
  between operations  13.3 us (3%)
  local copies, waits for them, and re-layouts  6.8 us (2%)
  matrix products  5.2 us (1%)
    psum x1, waiting for transfers between devices, one_after_other(): return lax.psum(partial, axis_two)  123 us
    psum x1, blocking collectives, one_after_other(): return lax.psum(partial, axis_two)  106 us
    pmax x1, blocking collectives, on_device(): peak_all = lax.pmax(req_top, ('group', 'tp'))  74 us
    unnamed x4, waiting for transfers between devices  40.7 us
    psum x1, blocking collectives, one_after_other(): partial = lax.psum(value, axis_one)  29 us
    all_gather x1, blocking collectives, on_device(): queries = lax.all_gather(qkv[:, :qdim], 'group', axis=0, tiled=True)  24.7 us
    all_gather x1, blocking collectives, on_device(): qkv = lax.all_gather(columns, 'tp', axis=1, tiled=True)  19.1 us
  transfers between devices with their start and end apart: 3, of which 2 were waited for; matrix products, arithmetic and copies ran while one was open for 0% of the time, Pallas kernels for 0%

profile of v1, /device:TPU:2, one launch (start us, length us, event | category | flops | bytes accessed | tf_op | source)
XLA Modules:
  0.0 444.8 jit_solution(15075103546881293483)
XLA Ops:
  6.5 1.1 fusion.1
  7.7 0.2 copy-done
  8.0 1.0 convolution_convert_fusion
  9.0 19.1 %all_gather.6 = bf16[2,2048]{1,0:T(2,128)(2,1)S(1)} all-gather(bf16[2,256]{1,0:T(2,128)(2,1)S(1)} %convolution_convert_fusion), channel_id=1, replica_groups=mesh['group'=32,'tp'=8] {'tp'}, dimensions={1}, use_global_device_ids=true | all-gather | bytes 9216 | tf_op jit(solution)/shard_map/all_gather | solution.py:25
  28.1 24.7 %all-gather = bf16[32,2,1536]{2,1,0:T(2,128)(2,1)S(1)} all-gather(bf16[1,2,1536]{2,1,0:T(2,128)(2,1)S(1)} %get-tuple-element.19), channel_id=1, replica_groups=mesh['group'=32,'tp'=8] {'group'}, dimensions={0}, use_global_device_ids=true | all-gather | bytes 202752 | tf_op jit(solution)/shard_map/all_gather | solution.py:26
  52.9 0.6 gather_fusion
  53.5 0.6 gather_fusion.1
  54.1 1.3 fusion.25
  55.4 0.3 copy.96
  55.8 0.3 select_reduce_fusion
  56.1 0.1 copy.81
  56.2 0.1 select_reduce_fusion.1
  56.3 0.1 copy.82
  56.4 0.3 copy.97
  56.7 0.2 convert_reduce_fusion
  56.9 0.1 copy.86
  57.0 74.0 %pmax.7 = f32[64,12]{1,0:T(8,128)S(1)} all-reduce(f32[64,12]{1,0:T(8,128)S(1)} %copy.86), channel_id=1, replica_groups=mesh['group'=32,'tp'=8] {'group','tp'}, use_global_device_ids=true, to_apply=%region_4.5 | all-reduce | flops 768 | bytes 6144 | tf_op jit(solution)/shard_map/pmax | solution.py:63
  131.0 0.6 gather_fusion.2
  131.6 0.2 fusion.5
  131.8 0.1 copy.88
  131.9 0.4 convolution_multiply_fusion
  132.3 0.4 fusion.2
  132.8 0.2 copy.84
  133.2 0.2 broadcast_in_dim.104
  133.3 0.9 bitcast_multiply_fusion
  134.4 0.1 fusion.27
  134.6 29.0 %psum.30 = f32[64,12]{1,0:T(8,128)S(1)} all-reduce(f32[64,12]{1,0:T(8,128)S(1)} %get-tuple-element.10), channel_id=1, replica_groups=mesh['group'=32,'tp'=8] {'tp'}, use_global_device_ids=true, to_apply=%region_8.9 | all-reduce | flops 768 | bytes 6144 | tf_op jit(solution)/shard_map/psum | solution.py:12
  163.6 106.3 %psum.31 = f32[64,12]{1,0:T(8,128)S(1)} all-reduce(f32[64,12]{1,0:T(8,128)S(1)} %psum.30), channel_id=1, replica_groups=mesh['group'=32,'tp'=8] {'group'}, use_global_device_ids=true, to_apply=%region_9.10 | all-reduce | flops 768 | bytes 6144 | tf_op jit(solution)/shard_map/psum | solution.py:13
  270.2 123.1 %all-reduce.5.cloned.1.call-done = f32[64,1536]{1,0:T(8,128)} async-done(((f32[64,1536]{1,0:T(8,128)}), f32[64,1536]{1,0:T(8,128)}) %all-reduce.5.cloned.1.call-update) | async-done | bytes 393232 | tf_op jit(solution)/shard_map/psum | solution.py:13
  393.3 2.7 convolution_bitcast_fusion
  396.0 40.6 %reduce-scatter.4.cloned.1.call-done = f32[384,2]{1,0:T(8,128)} async-done(((f32[3072,2]{1,0:T(8,128)}), f32[384,2]{1,0:T(8,128)}) %reduce-scatter.4.cloned.1.call-update) | async-done | bytes 3088
  436.6 1.6 copy.95
  (39 shorter events, 0.9 us)
Async XLA Ops:
  6.5 1.4 copy-start
  6.5 46.4 %copy-start.1 = (s32[64]{0:T(128)S(1)}, s32[64]{0:T(128)}, u32[]{:S(2)}) copy-start(s32[64]{0:T(128)} %param.11) | copy-start | bytes 772
  6.5 263.5 %all-reduce.3.cloned.1.call-start = ((), (), s32[]{:S(2)}) async-start(), calls=%async_computation.1 | async-start | bytes 786432 | tf_op jit(solution)/shard_map/psum | solution.py:12
  133.1 260.2 %copy-start.2 = (bf16[192,3072]{1,0:T(8,128)(2,1)S(1)}, bf16[192,3072]{1,0:T(8,128)(2,1)}, u32[]{:S(2)}) copy-start(bf16[192,3072]{1,0:T(8,128)(2,1)} %param.8) | copy-start | bytes 3538948
  134.3 259.0 %all-reduce.5.cloned.1.call-start = ((), (), s32[]{:S(2)}) async-start(), calls=%async_computation.2 | async-start | bytes 786432 | tf_op jit(solution)/shard_map/psum | solution.py:13
  270.0 166.6 %reduce-scatter.4.cloned.1.call-start = ((), (), s32[]{:S(2)}) async-start(), calls=%async_computation.3 | async-start | bytes 1769472
Sparse Core Ops, SparseCore 0:
  134.4 69.0 all-reduce.2
  270.2 123.0 all-reduce.4
  396.1 40.4 reduce-scatter.3
